TPU v7x, 32 devices: a whole 2x2x4 slice. The times are simulated.
32 devices in a mesh: gx: 4 (over y, x), gy: 8 (over z, core).
Axes of the slice: x: 2, y: 2, z: 4, core: 2. Of those that a mesh axis runs over, the one named last changes fastest.
Arguments:
- material: int32 [8, 128, 512], P('gx', 'gy'), may hold values from 0 to 3
- phase: int32 [8, 128, 512], P('gx', 'gy'), may hold values from 0 to 7
- clock: float32 [1], replicated, may hold values from -3.140625 to 3.140625
- displacement: float32 [3, 8, 128, 512], P(None, 'gx', 'gy'), may hold values from -6 to 6
- velocity: float32 [3, 8, 128, 512], P(None, 'gx', 'gy'), may hold values from -6 to 6
- cotangent: float32 [3, 8, 128, 512], P(None, 'gx', 'gy'), may hold values from -4 to 4
- material_table: float32 [2, 4], replicated, may hold values from 0.5 to 4
- w_in: bfloat16 [256, 10], replicated, may hold values from -2 to 2
- b_in: float32 [256], replicated, may hold values from -3 to 3
- w_mid: bfloat16 [2, 256, 256], replicated, may hold values from -0.375 to 0.375
- b_mid: float32 [2, 256], replicated, may hold values from -3 to 3
- w_out: bfloat16 [9, 256], replicated, may hold values from -0.375 to 0.375
- b_out: float32 [9], replicated, may hold values from -3 to 3
Outputs:
- velocity_new: float32 [3, 8, 128, 512], P(None, 'gx', 'gy')
- displacement_grad: float32 [3, 8, 128, 512], P(None, 'gx', 'gy')
- grad_w_in: float32 [256, 10], replicated
- grad_b_in: float32 [256], replicated
- grad_w_mid: float32 [2, 256, 256], replicated
- grad_b_mid: float32 [2, 256], replicated
- grad_w_out: float32 [9, 256], replicated
- grad_b_out: float32 [9], replicated
All inputs are finite; a program needn't handle non-finite values.
Results may differ from a plain program's by a relative error of at most 0.02.
Values sent between devices are 32-bit elements; how exact they have to be, the bound alone decides.
No kernel may reach another device: no remote copies, remote signals or barrier semaphores. Data moves between devices by JAX's collectives and lax.ppermute only.
A program may use at most 64 MiB of HBM per device.

v0:
```python
import jax
import jax.numpy as jnp
from jax import lax
from jax.sharding import PartitionSpec as P

FEAT = 10
OUT = 9
PHASES = 8
NPARAM = 136713
time_step = 0.25
viscosity = 0.2
norm_eps = 1e-06
two_pi = 6.283185307179586


def with_halo(block, sides, width):
    for axis, dim in sides:
        count = lax.axis_size(axis)
        forward = [(i, i + 1) for i in range(count - 1)]
        backward = [(target, source) for source, target in forward]
        low = lax.ppermute(
            lax.slice_in_dim(block, block.shape[dim] - width, None, axis=dim), axis, forward
        )
        high = lax.ppermute(lax.slice_in_dim(block, 0, width, axis=dim), axis, backward)
        block = jnp.concatenate([low, block, high], axis=dim)
    return block


def zdiff(field):
    padded = jnp.pad(field, ((0, 0), (0, 0), (0, 0), (1, 1)))
    return (padded[..., 2:] - padded[..., :-2]) * 0.5


def xdiff_both(padded):
    return (padded[:, 2:, 1:-1] - padded[:, :-2, 1:-1]) * 0.5


def ydiff_both(padded):
    return (padded[:, 1:-1, 2:] - padded[:, 1:-1, :-2]) * 0.5


def forward_block(feats, w_in, b_in, w_mid, b_mid, w_out, b_out):
    first = jnp.tanh(
        jnp.dot(w_in, feats, preferred_element_type=jnp.float32) + b_in[:, None]
    ).astype(jnp.bfloat16)
    second = jnp.tanh(
        jnp.dot(w_mid[0], first, preferred_element_type=jnp.float32) + b_mid[0][:, None]
    ).astype(jnp.bfloat16)
    third = jnp.tanh(
        jnp.dot(w_mid[1], second, preferred_element_type=jnp.float32) + b_mid[1][:, None]
    ).astype(jnp.bfloat16)
    result = jnp.dot(w_out, third, preferred_element_type=jnp.float32) + b_out[:, None]
    return (first, second, third, result)


def backward_block(feats, delta, w_in, b_in, w_mid, b_mid, w_out, b_out):
    first, second, third, result = forward_block(feats, w_in, b_in, w_mid, b_mid, w_out, b_out)
    delta_out = delta.astype(jnp.bfloat16)
    grad_wout = jnp.dot(delta_out, third.T, preferred_element_type=jnp.float32)
    grad_bout = jnp.sum(delta_out.astype(jnp.float32), axis=1)
    back_third = jnp.dot(w_out.T, delta_out, preferred_element_type=jnp.float32)
    delta_third = (back_third * (1.0 - jnp.square(third.astype(jnp.float32)))).astype(jnp.bfloat16)
    grad_wthree = jnp.dot(delta_third, second.T, preferred_element_type=jnp.float32)
    grad_bthree = jnp.sum(delta_third.astype(jnp.float32), axis=1)
    back_second = jnp.dot(w_mid[1].T, delta_third, preferred_element_type=jnp.float32)
    delta_second = (back_second * (1.0 - jnp.square(second.astype(jnp.float32)))).astype(
        jnp.bfloat16
    )
    grad_wtwo = jnp.dot(delta_second, first.T, preferred_element_type=jnp.float32)
    grad_btwo = jnp.sum(delta_second.astype(jnp.float32), axis=1)
    back_first = jnp.dot(w_mid[0].T, delta_second, preferred_element_type=jnp.float32)
    delta_first = (back_first * (1.0 - jnp.square(first.astype(jnp.float32)))).astype(jnp.bfloat16)
    grad_win = jnp.dot(delta_first, feats.T, preferred_element_type=jnp.float32)
    grad_bin = jnp.sum(delta_first.astype(jnp.float32), axis=1)
    back_feats = jnp.dot(w_in.T, delta_first, preferred_element_type=jnp.float32)
    grads = (
        grad_win,
        grad_bin,
        jnp.stack([grad_wtwo, grad_wthree]),
        jnp.stack([grad_btwo, grad_bthree]),
        grad_wout,
        grad_bout,
    )
    return (grads, back_feats, result)


def body(
    material,
    phase,
    clock,
    displacement,
    velocity,
    cotangent,
    material_table,
    w_in,
    b_in,
    w_mid,
    b_mid,
    w_out,
    b_out,
):
    size_x, size_y, size_z = material.shape
    kinds = jnp.arange(material_table.shape[1], dtype=jnp.int32)
    onehot = (material[None] == kinds[:, None, None, None]).astype(jnp.float32)
    stiffness = jnp.tensordot(material_table[0], onehot, axes=1)
    density = jnp.tensordot(material_table[1], onehot, axes=1)
    occupied = (material > 0).astype(jnp.float32)
    actuation = jnp.sin(two_pi * phase.astype(jnp.float32) / PHASES + clock[0])
    carried = time_step * occupied * cotangent / density
    rims = with_halo(jnp.concatenate([displacement, velocity], 0), (("gx", 1), ("gy", 2)), 1)
    disp_rim = rims[0:3]
    velo_rim = rims[3:6]
    strain = jnp.stack(
        [xdiff_both(disp_rim), ydiff_both(disp_rim), zdiff(displacement)], axis=1
    ).reshape(9, size_x, size_y, size_z)
    feats = jnp.concatenate([strain, actuation[None]], 0).reshape(FEAT, -1).astype(jnp.bfloat16)
    voxels = size_x * size_y * size_z
    block_rows = min(2048, voxels)
    count = voxels // block_rows
    feat_blocks = feats.reshape(FEAT, count, block_rows).transpose(1, 0, 2)
    weights = (w_in, b_in, w_mid, b_mid, w_out, b_out)
    carried_rim = with_halo(carried, (("gx", 1), ("gy", 2)), 1)
    stress_grad = -jnp.stack(
        [xdiff_both(carried_rim), ydiff_both(carried_rim), zdiff(carried)], axis=1
    ).reshape(9, size_x, size_y, size_z)
    delta_all = (
        (occupied * stiffness * stress_grad).reshape(OUT, count, block_rows).transpose(1, 0, 2)
    )
    zeros = (
        jnp.zeros(w_in.shape, jnp.float32),
        jnp.zeros(b_in.shape, jnp.float32),
        jnp.zeros(w_mid.shape, jnp.float32),
        jnp.zeros(b_mid.shape, jnp.float32),
        jnp.zeros(w_out.shape, jnp.float32),
        jnp.zeros(b_out.shape, jnp.float32),
    )

    def backward_step(carry, pieces):
        grads, back_feats, result = backward_block(pieces[0], pieces[1], *weights)
        return (
            jax.tree.map(lambda left, right: left + right, carry, grads),
            (back_feats[:9], result),
        )

    partials, (back_blocks, outputs) = lax.scan(backward_step, zeros, (feat_blocks, delta_all))
    network = outputs.transpose(1, 0, 2).reshape(OUT, size_x, size_y, size_z)
    stress = (occupied * stiffness * network).reshape(3, 3, size_x, size_y, size_z)
    stress_x = with_halo(stress[:, 0], (("gx", 1),), 1)
    stress_y = with_halo(stress[:, 1], (("gy", 2),), 1)
    force = (
        (stress_x[:, 2:] - stress_x[:, :-2]) * 0.5
        + (stress_y[:, :, 2:] - stress_y[:, :, :-2]) * 0.5
        + zdiff(stress[:, 2])
    )
    inner = velo_rim[:, 1:-1, 1:-1]
    lap_z = jnp.pad(velocity, ((0, 0), (0, 0), (0, 0), (1, 1)))
    laplacian = -6.0 * velocity
    laplacian = laplacian + velo_rim[:, 2:, 1:-1] + velo_rim[:, :-2, 1:-1]
    laplacian = laplacian + velo_rim[:, 1:-1, 2:] + velo_rim[:, 1:-1, :-2]
    laplacian = laplacian + lap_z[..., 2:] + lap_z[..., :-2]
    velocity_new = inner + time_step * occupied * (force + viscosity * laplacian) / density
    strain_grad = back_blocks.transpose(1, 0, 2).reshape(3, 3, size_x, size_y, size_z)
    back_x = with_halo(strain_grad[:, 0], (("gx", 1),), 1)
    back_y = with_halo(strain_grad[:, 1], (("gy", 2),), 1)
    displacement_grad = -(
        (back_x[:, 2:] - back_x[:, :-2]) * 0.5
        + (back_y[:, :, 2:] - back_y[:, :, :-2]) * 0.5
        + zdiff(strain_grad[:, 2])
    )
    summed = lax.psum(
        (partials[0], partials[1], partials[2], partials[3], partials[4], partials[5]), ("gx", "gy")
    )
    total = sum((jnp.sum(jnp.square(item)) for item in summed))
    scale = lax.rsqrt(total / NPARAM + norm_eps)
    results = tuple((item * scale for item in summed))
    return (
        velocity_new,
        displacement_grad,
        results[0],
        results[1],
        results[2],
        results[3],
        results[4],
        results[5],
    )


def solution(mesh):
    in_specs = (
        P("gx", "gy", None),
        P("gx", "gy", None),
        P(),
        P(None, "gx", "gy", None),
        P(None, "gx", "gy", None),
        P(None, "gx", "gy", None),
        P(),
        P(),
        P(),
        P(),
        P(),
        P(),
        P(),
    )
    out_specs = (P(None, "gx", "gy", None), P(None, "gx", "gy", None), P(), P(), P(), P(), P(), P())
    return jax.shard_map(body, mesh=mesh, in_specs=in_specs, out_specs=out_specs, check_vma=False)
```

profile of v0, /device:TPU:0, one launch (start us, length us, event | category | flops | bytes accessed | tf_op | source)
XLA Modules:
  0.0 267.0 jit_solution(9475212293226691999)
XLA Ops:
  7.2 0.9 iota_compare_fusion
  8.2 0.9 fusion.70
  9.1 0.9 fusion.72
  10.2 4.8 %collective-permute-start.1 = (f32[3,1,16,512]{3,2,1,0:T(8,128)S(1)}, f32[3,1,16,512]{3,2,1,0:T(8,128)S(1)}, u32[]{:S(2)}, u32[]{:S(2)}) collective-permute-start(f32[3,1,16,512]{3,2,1,0:T(8,128)S(1)} %get-tuple-element.257), channel_id=1, source_target_pairs={{0,8},{8,16},{16,24},{1,9},{9,17},{17,25},{2,10},{10,18},{18,26},{... | collective-permute-start | bytes 294920 | tf_op jit(solution)/shard_map/ppermute | solution.py:21
  15.1 1.4 collective-permute-start
  16.6 0.8 constant_dynamic-update-slice_fusion.1
  17.4 0.8 fusion.78
  18.2 4.5 %collective-permute-start.5 = (f32[6,1,16,512]{3,2,1,0:T(8,128)}, f32[6,1,16,512]{3,2,1,0:T(8,128)S(1)}, u32[]{:S(2)}, u32[]{:S(2)}) collective-permute-start(f32[6,1,16,512]{3,2,1,0:T(8,128)} %get-tuple-element.240), channel_id=1, source_target_pairs={{0,8},{8,16},{16,24},{1,9},{9,17},{17,25},{2,10},{10,18},{18,26},{... | collective-permute-start | bytes 589832 | tf_op jit(solution)/shard_map/ppermute | solution.py:21
  22.7 1.3 collective-permute-start.4
  24.8 1.3 collective-permute-start.2
  26.1 3.0 %collective-permute-start.3 = (f32[3,4,1,512]{3,2,1,0:T(1,128)S(1)}, f32[3,4,1,512]{3,2,1,0:T(1,128)S(1)}, u32[]{:S(2)}, u32[]{:S(2)}) collective-permute-start(f32[3,4,1,512]{3,2,1,0:T(1,128)S(1)} %get-tuple-element.245), channel_id=1, source_target_pairs={{0,1},{1,2},{2,3},{3,4},{4,5},{5,6},{6,7},{8,9},{9,10},{10,11},{11... | collective-permute-start | bytes 73736 | tf_op jit(solution)/shard_map/ppermute | solution.py:21
  30.1 0.7 mul.133
  31.3 2.3 collective-permute-done.4
  33.7 1.4 collective-permute-start.6
  35.1 3.0 %collective-permute-start.7 = (f32[6,4,1,512]{3,2,1,0:T(1,128)S(1)}, f32[6,4,1,512]{3,2,1,0:T(1,128)S(1)}, u32[]{:S(2)}, u32[]{:S(2)}) collective-permute-start(f32[6,4,1,512]{3,2,1,0:T(1,128)S(1)} %get-tuple-element.233), channel_id=1, source_target_pairs={{0,1},{1,2},{2,3},{3,4},{4,5},{5,6},{6,7},{8,9},{9,10},{10,11},{11... | collective-permute-start | bytes 147464 | tf_op jit(solution)/shard_map/ppermute | solution.py:21
  38.1 0.9 multiply_bitcast_fusion
  40.5 76.0 %while.25 = (s32[]{:T(128)}, f32[256,10]{0,1:T(8,128)S(1)}, f32[256]{0:T(256)}, f32[2,256,256]{2,1,0:T(8,128)S(1)}, f32[2,256]{1,0:T(2,128)}, /*index=5*/f32[9,2...) while((s32[]{:T(128)}, f32[256,10]{0,1:T(8,128)S(1)}, ...), condition=%wide.region_5.6_spmd.clone, body=%wide.region_0.5_spmd.clone.sunk | while | flops 1684996864 | bytes 26539676 | solution.py:145
  40.5 0.8 fusion.150
  42.0 1.2 fusion.149
  48.8 0.7 fusion.154
  49.4 0.8 fusion.150
  50.4 1.2 fusion.153
  51.6 1.2 fusion.149
  58.3 0.7 fusion.154
  59.0 0.8 fusion.150
  60.0 1.2 fusion.153
  61.2 1.2 fusion.149
  67.9 0.7 fusion.154
  68.6 0.8 fusion.150
  69.6 1.2 fusion.153
  70.8 1.2 fusion.149
  77.5 0.7 fusion.154
  78.2 0.8 fusion.150
  79.2 1.2 fusion.153
  80.3 1.2 fusion.149
  87.1 0.7 fusion.154
  87.8 0.8 fusion.150
  88.7 1.2 fusion.153
  89.9 1.2 fusion.149
  96.7 0.7 fusion.154
  97.3 0.8 fusion.150
  98.3 1.2 fusion.153
  99.5 1.2 fusion.149
  106.2 0.7 fusion.154
  106.9 0.8 fusion.150
  107.9 1.2 fusion.153
  109.1 1.2 fusion.149
  115.8 0.7 fusion.154
  118.5 1.3 collective-permute-start.10
  119.9 44.8 %all-reduce.5 = (f32[256,10]{0,1:T(8,128)S(1)}, f32[256]{0:T(256)S(1)}, f32[2,256]{1,0:T(2,128)S(1)}, f32[9,256]{1,0:T(8,128)S(1)}, f32[9]{0:T(128)S(1)}) all-reduce(f32[256,10]{0,1:T(8,128)S(1)} %copy-done.11, f32[256]{0:T(256)S(1)} %copy-done.29, f32[2,256]{1,0:T(2,128)S(1)} %copy-done.25, ...), channel_id=1, replica_groups=mesh['gx'=4,'gy'=8] {'gx','gy'}, use_global_device_ids=true, to_apply=%region_6.7 | all-reduce | flops 5641 | bytes 45128 | tf_op jit(solution)/shard_map/psum | solution.py:170
  167.1 1.6 copy.28
  169.0 1.4 collective-permute-start.14
  170.4 3.0 %collective-permute-start.15 = (f32[3,2,1,512]{3,2,1,0:T(1,128)S(1)}, f32[3,2,1,512]{3,2,1,0:T(1,128)S(1)}, u32[]{:S(2)}, u32[]{:S(2)}) collective-permute-start(f32[3,2,1,512]{3,2,1,0:T(1,128)S(1)} %get-tuple-element.249), channel_id=1, source_target_pairs={{0,1},{1,2},{2,3},{3,4},{4,5},{5,6},{6,7},{8,9},{9,10},{10,11},{11... | collective-permute-start | bytes 36872 | tf_op jit(solution)/shard_map/ppermute | solution.py:21
  173.5 1.3 collective-permute-start.12
  174.8 4.8 %collective-permute-start.13 = (f32[3,1,16,512]{3,2,1,0:T(8,128)S(1)}, f32[3,1,16,512]{3,2,1,0:T(8,128)S(1)}, u32[]{:S(2)}, u32[]{:S(2)}) collective-permute-start(f32[3,1,16,512]{3,2,1,0:T(8,128)S(1)} %get-tuple-element.247), channel_id=1, source_target_pairs={{0,8},{8,16},{16,24},{1,9},{9,17},{17,25},{2,10},{10,18},{18,26},{... | collective-permute-start | bytes 294920 | tf_op jit(solution)/shard_map/ppermute | solution.py:21
  181.4 2.7 %collective-permute-start.11 = (f32[3,2,1,512]{3,2,1,0:T(1,128)S(1)}, f32[3,2,1,512]{3,2,1,0:T(1,128)S(1)}, u32[]{:S(2)}, u32[]{:S(2)}) collective-permute-start(f32[3,2,1,512]{3,2,1,0:T(1,128)S(1)} %get-tuple-element.253), channel_id=1, source_target_pairs={{0,1},{1,2},{2,3},{3,4},{4,5},{5,6},{6,7},{8,9},{9,10},{10,11},{11... | collective-permute-start | bytes 36872 | tf_op jit(solution)/shard_map/ppermute | solution.py:21
  184.2 1.3 collective-permute-start.8
  185.5 5.2 %collective-permute-start.9 = (f32[3,1,16,512]{3,2,1,0:T(8,128)S(1)}, f32[3,1,16,512]{3,2,1,0:T(8,128)S(1)}, u32[]{:S(2)}, u32[]{:S(2)}) collective-permute-start(f32[3,1,16,512]{3,2,1,0:T(8,128)S(1)} %get-tuple-element.251), channel_id=1, source_target_pairs={{0,8},{8,16},{16,24},{1,9},{9,17},{17,25},{2,10},{10,18},{18,26},{... | collective-permute-start | bytes 294920 | tf_op jit(solution)/shard_map/ppermute | solution.py:21
  190.7 0.9 fusion.49
  192.1 1.8 collective-permute-done.9
  193.9 1.0 fusion.42
  194.8 56.2 %all-reduce.8.cloned.1.call-done = f32[2,256,256]{2,1,0:T(8,128)} async-done(((f32[2,256,256]{2,1,0:T(8,128)}), f32[2,256,256]{2,1,0:T(8,128)}) %all-reduce.8.cloned.1.call-update) | async-done | bytes 524304 | tf_op jit(solution)/shard_map/psum | solution.py:170
  251.0 1.8 multiply_reduce_fusion
  258.3 1.9 broadcast_multiply_fusion.1
  (343 shorter events, 57.9 us)
Async XLA Ops:
  7.2 2.9 %copy-start.13 = (s32[2,16,512]{2,1,0:T(8,128)S(1)}, s32[2,16,512]{2,1,0:T(8,128)}, u32[]{:S(2)}) copy-start(s32[2,16,512]{2,1,0:T(8,128)} %param.15) | copy-start | bytes 196612
  7.2 3.0 %copy-start.20 = (f32[3,2,16,512]{3,2,1,0:T(8,128)S(1)}, f32[3,2,16,512]{3,2,1,0:T(8,128)}, u32[]{:S(2)}) copy-start(f32[3,2,16,512]{3,2,1,0:T(8,128)} %param.20) | copy-start | bytes 589828
  7.2 243.8 %all-reduce.8.cloned.1.call-start = ((), (), s32[]{:S(2)}) async-start(), calls=%async_computation | async-start | bytes 1048576 | tf_op jit(solution)/shard_map/psum | solution.py:170
  8.2 8.4 %copy-start.21 = (f32[3,2,16,512]{3,2,1,0:T(8,128)S(1)}, f32[3,2,16,512]{3,2,1,0:T(8,128)}, u32[]{:S(2)}) copy-start(f32[3,2,16,512]{3,2,1,0:T(8,128)} %param.18) | copy-start | bytes 589828
  9.1 8.3 %copy-start.1 = (f32[3,2,16,512]{3,2,1,0:T(8,128)S(1)}, f32[3,2,16,512]{3,2,1,0:T(8,128)}, u32[]{:S(2)}) copy-start(f32[3,2,16,512]{3,2,1,0:T(8,128)} %param.19) | copy-start | bytes 589828
  10.1 5.0 %copy-start.7 = (f32[1,2,16,512]{3,2,1,0:T(8,128)}, f32[1,2,16,512]{3,2,1,0:T(8,128)S(1)}, u32[]{:S(2)}) copy-start(f32[1,2,16,512]{3,2,1,0:T(8,128)S(1)} %copy.58) | copy-start | bytes 196612
  10.1 19.9 %copy-start.3 = (f32[2,16,512]{2,1,0:T(8,128)}, f32[2,16,512]{2,1,0:T(8,128)S(1)}, u32[]{:S(2)}) copy-start(f32[2,16,512]{2,1,0:T(8,128)S(1)} %get-tuple-element.220) | copy-start | bytes 196612
  10.2 5.0 %copy-start.5 = (f32[2,16,512]{2,1,0:T(8,128)}, f32[2,16,512]{2,1,0:T(8,128)S(1)}, u32[]{:S(2)}) copy-start(f32[2,16,512]{2,1,0:T(8,128)S(1)} %broadcast_select_fusion.1) | copy-start | bytes 196612
  10.2 14.4 %collective-permute-start.1 = (f32[3,1,16,512]{3,2,1,0:T(8,128)S(1)}, f32[3,1,16,512]{3,2,1,0:T(8,128)S(1)}, u32[]{:S(2)}, u32[]{:S(2)}) collective-permute-start(f32[3,1,16,512]{3,2,1,0:T(8,128)S(1)} %get-tuple-element.257), channel_id=1, source_target_pairs={{0,8},{8,16},{16,24},{1,9},{9,17},{17,25},{2,10},{10,18},{18,26},{... | collective-permute-start | bytes 294920 | tf_op jit(solution)/shard_map/ppermute | solution.py:21
  15.1 14.0 %copy-start.26 = (s32[2,16,512]{2,1,0:T(8,128)S(1)}, s32[2,16,512]{2,1,0:T(8,128)}, u32[]{:S(2)}) copy-start(s32[2,16,512]{2,1,0:T(8,128)} %param.16) | copy-start | bytes 196612
  15.1 9.6 %collective-permute-start = (f32[3,1,16,512]{3,2,1,0:T(8,128)S(1)}, f32[3,1,16,512]{3,2,1,0:T(8,128)S(1)}, u32[]{:S(2)}, u32[]{:S(2)}) collective-permute-start(f32[3,1,16,512]{3,2,1,0:T(8,128)S(1)} %get-tuple-element.258), channel_id=1, source_target_pairs={{8,0},{16,8},{24,16},{9,1},{17,9},{25,17},{10,2},{18,10},{26,18},{... | collective-permute-start | bytes 294920 | tf_op jit(solution)/shard_map/ppermute | solution.py:24
  18.2 13.1 %collective-permute-start.5 = (f32[6,1,16,512]{3,2,1,0:T(8,128)}, f32[6,1,16,512]{3,2,1,0:T(8,128)S(1)}, u32[]{:S(2)}, u32[]{:S(2)}) collective-permute-start(f32[6,1,16,512]{3,2,1,0:T(8,128)} %get-tuple-element.240), channel_id=1, source_target_pairs={{0,8},{8,16},{16,24},{1,9},{9,17},{17,25},{2,10},{10,18},{18,26},{... | collective-permute-start | bytes 589832 | tf_op jit(solution)/shard_map/ppermute | solution.py:21
  22.7 10.8 %collective-permute-start.4 = (f32[6,1,16,512]{3,2,1,0:T(8,128)}, f32[6,1,16,512]{3,2,1,0:T(8,128)S(1)}, u32[]{:S(2)}, u32[]{:S(2)}) collective-permute-start(f32[6,1,16,512]{3,2,1,0:T(8,128)} %get-tuple-element.241), channel_id=1, source_target_pairs={{8,0},{16,8},{24,16},{9,1},{17,9},{25,17},{10,2},{18,10},{26,18},{... | collective-permute-start | bytes 589832 | tf_op jit(solution)/shard_map/ppermute | solution.py:24
  24.8 6.0 %collective-permute-start.2 = (f32[3,4,1,512]{3,2,1,0:T(1,128)S(1)}, f32[3,4,1,512]{3,2,1,0:T(1,128)S(1)}, u32[]{:S(2)}, u32[]{:S(2)}) collective-permute-start(f32[3,4,1,512]{3,2,1,0:T(1,128)S(1)} %get-tuple-element.244), channel_id=1, source_target_pairs={{1,0},{2,1},{3,2},{4,3},{5,4},{6,5},{7,6},{9,8},{10,9},{11,10},{12... | collective-permute-start | bytes 73736 | tf_op jit(solution)/shard_map/ppermute | solution.py:24
  26.1 4.7 %collective-permute-start.3 = (f32[3,4,1,512]{3,2,1,0:T(1,128)S(1)}, f32[3,4,1,512]{3,2,1,0:T(1,128)S(1)}, u32[]{:S(2)}, u32[]{:S(2)}) collective-permute-start(f32[3,4,1,512]{3,2,1,0:T(1,128)S(1)} %get-tuple-element.245), channel_id=1, source_target_pairs={{0,1},{1,2},{2,3},{3,4},{4,5},{5,6},{6,7},{8,9},{9,10},{10,11},{11... | collective-permute-start | bytes 73736 | tf_op jit(solution)/shard_map/ppermute | solution.py:21
  33.7 6.0 %copy-start.12 = (bf16[3,1,2,16,512]{4,3,2,0,1:T(8,128)(2,1)S(1)}, bf16[3,1,2,16,512]{4,3,2,0,1:T(8,128)(2,1)}, u32[]{:S(2)}) copy-start(bf16[3,1,2,16,512]{4,3,2,0,1:T(8,128)(2,1)} %get-tuple-element.255) | copy-start | bytes 294916
  33.7 5.4 %collective-permute-start.6 = (f32[6,4,1,512]{3,2,1,0:T(1,128)S(1)}, f32[6,4,1,512]{3,2,1,0:T(1,128)S(1)}, u32[]{:S(2)}, u32[]{:S(2)}) collective-permute-start(f32[6,4,1,512]{3,2,1,0:T(1,128)S(1)} %get-tuple-element.232), channel_id=1, source_target_pairs={{1,0},{2,1},{3,2},{4,3},{5,4},{6,5},{7,6},{9,8},{10,9},{11,10},{12... | collective-permute-start | bytes 147464 | tf_op jit(solution)/shard_map/ppermute | solution.py:24
  35.1 3.9 %collective-permute-start.7 = (f32[6,4,1,512]{3,2,1,0:T(1,128)S(1)}, f32[6,4,1,512]{3,2,1,0:T(1,128)S(1)}, u32[]{:S(2)}, u32[]{:S(2)}) collective-permute-start(f32[6,4,1,512]{3,2,1,0:T(1,128)S(1)} %get-tuple-element.233), channel_id=1, source_target_pairs={{0,1},{1,2},{2,3},{3,4},{4,5},{5,6},{6,7},{8,9},{9,10},{10,11},{11... | collective-permute-start | bytes 147464 | tf_op jit(solution)/shard_map/ppermute | solution.py:21
  39.2 0.8 copy-start.22
  39.8 0.7 copy-start.9
  39.8 0.7 copy-start.14
  39.8 0.7 copy-start.15
  40.5 2.7 %copy-start.32 = (bf16[2,256,256]{2,1,0:T(8,128)(2,1)S(1)}, bf16[2,256,256]{2,1,0:T(8,128)(2,1)}, u32[]{:S(2)}) copy-start(bf16[2,256,256]{2,1,0:T(8,128)(2,1)} %get-tuple-element.430) | copy-start | bytes 786436 | tf_op jit(solution)/shard_map/while
  45.9 0.7 copy-start.23
  46.6 1.1 copy-start.24
  49.4 3.3 %copy-start.32 = (bf16[2,256,256]{2,1,0:T(8,128)(2,1)S(1)}, bf16[2,256,256]{2,1,0:T(8,128)(2,1)}, u32[]{:S(2)}) copy-start(bf16[2,256,256]{2,1,0:T(8,128)(2,1)} %get-tuple-element.430) | copy-start | bytes 786436 | tf_op jit(solution)/shard_map/while
  55.5 0.7 copy-start.23
  56.2 1.1 copy-start.24
  59.0 3.3 %copy-start.32 = (bf16[2,256,256]{2,1,0:T(8,128)(2,1)S(1)}, bf16[2,256,256]{2,1,0:T(8,128)(2,1)}, u32[]{:S(2)}) copy-start(bf16[2,256,256]{2,1,0:T(8,128)(2,1)} %get-tuple-element.430) | copy-start | bytes 786436 | tf_op jit(solution)/shard_map/while
  65.1 0.7 copy-start.23
  65.8 1.1 copy-start.24
  68.6 3.3 %copy-start.32 = (bf16[2,256,256]{2,1,0:T(8,128)(2,1)S(1)}, bf16[2,256,256]{2,1,0:T(8,128)(2,1)}, u32[]{:S(2)}) copy-start(bf16[2,256,256]{2,1,0:T(8,128)(2,1)} %get-tuple-element.430) | copy-start | bytes 786436 | tf_op jit(solution)/shard_map/while
  74.7 0.7 copy-start.23
  75.4 1.1 copy-start.24
  78.2 3.3 %copy-start.32 = (bf16[2,256,256]{2,1,0:T(8,128)(2,1)S(1)}, bf16[2,256,256]{2,1,0:T(8,128)(2,1)}, u32[]{:S(2)}) copy-start(bf16[2,256,256]{2,1,0:T(8,128)(2,1)} %get-tuple-element.430) | copy-start | bytes 786436 | tf_op jit(solution)/shard_map/while
  84.3 0.7 copy-start.23
  85.0 1.1 copy-start.24
  87.8 3.4 %copy-start.32 = (bf16[2,256,256]{2,1,0:T(8,128)(2,1)S(1)}, bf16[2,256,256]{2,1,0:T(8,128)(2,1)}, u32[]{:S(2)}) copy-start(bf16[2,256,256]{2,1,0:T(8,128)(2,1)} %get-tuple-element.430) | copy-start | bytes 786436 | tf_op jit(solution)/shard_map/while
  93.8 0.7 copy-start.23
  94.5 1.1 copy-start.24
  97.3 3.3 %copy-start.32 = (bf16[2,256,256]{2,1,0:T(8,128)(2,1)S(1)}, bf16[2,256,256]{2,1,0:T(8,128)(2,1)}, u32[]{:S(2)}) copy-start(bf16[2,256,256]{2,1,0:T(8,128)(2,1)} %get-tuple-element.430) | copy-start | bytes 786436 | tf_op jit(solution)/shard_map/while
  103.4 0.7 copy-start.23
  104.1 1.1 copy-start.24
  106.9 3.4 %copy-start.32 = (bf16[2,256,256]{2,1,0:T(8,128)(2,1)S(1)}, bf16[2,256,256]{2,1,0:T(8,128)(2,1)}, u32[]{:S(2)}) copy-start(bf16[2,256,256]{2,1,0:T(8,128)(2,1)} %get-tuple-element.430) | copy-start | bytes 786436 | tf_op jit(solution)/shard_map/while
  113.7 1.1 copy-start.24
  116.5 1.1 copy-start
  117.4 0.8 copy-start.4
  118.4 1.5 copy-start.11
  118.4 1.5 copy-start.25
  118.4 1.5 copy-start.29
  118.4 1.5 copy-start.30
  118.5 73.0 %collective-permute-start.10 = (f32[3,2,1,512]{3,2,1,0:T(1,128)S(1)}, f32[3,2,1,512]{3,2,1,0:T(1,128)S(1)}, u32[]{:S(2)}, u32[]{:S(2)}) collective-permute-start(f32[3,2,1,512]{3,2,1,0:T(1,128)S(1)} %get-tuple-element.252), channel_id=1, source_target_pairs={{1,0},{2,1},{3,2},{4,3},{5,4},{6,5},{7,6},{9,8},{10,9},{11,10},{12... | collective-permute-start | bytes 36872 | tf_op jit(solution)/shard_map/ppermute | solution.py:24
  168.8 25.0 %copy-start.2 = (f32[3,2,16,512]{3,2,1,0:T(8,128)S(1)}, f32[3,2,16,512]{3,2,1,0:T(8,128)}, u32[]{:S(2)}) copy-start(f32[3,2,16,512]{3,2,1,0:T(8,128)} %param.19) | copy-start | bytes 589828
  168.8 25.0 %copy-start.6 = (f32[2,16,512]{2,1,0:T(8,128)S(1)}, f32[2,16,512]{2,1,0:T(8,128)}, u32[]{:S(2)}) copy-start(f32[2,16,512]{2,1,0:T(8,128)} %copy-done.5) | copy-start | bytes 196612
  168.8 25.0 %copy-start.8 = (f32[1,2,16,512]{3,2,1,0:T(8,128)S(1)}, f32[1,2,16,512]{3,2,1,0:T(8,128)}, u32[]{:S(2)}) copy-start(f32[1,2,16,512]{3,2,1,0:T(8,128)} %copy-done.7) | copy-start | bytes 196612
  168.9 25.0 %copy-start.17 = (f32[6,4,1,512]{3,2,1,0:T(1,128)S(1)}, f32[6,4,1,512]{3,2,1,0:T(1,128)}, u32[]{:S(2)}) copy-start(f32[6,4,1,512]{3,2,1,0:T(1,128)} %copy-done.16) | copy-start | bytes 147460
  168.9 25.0 %copy-start.19 = (f32[6,4,1,512]{3,2,1,0:T(1,128)S(1)}, f32[6,4,1,512]{3,2,1,0:T(1,128)}, u32[]{:S(2)}) copy-start(f32[6,4,1,512]{3,2,1,0:T(1,128)} %copy-done.18) | copy-start | bytes 147460
  169.0 12.5 %collective-permute-start.14 = (f32[3,2,1,512]{3,2,1,0:T(1,128)S(1)}, f32[3,2,1,512]{3,2,1,0:T(1,128)S(1)}, u32[]{:S(2)}, u32[]{:S(2)}) collective-permute-start(f32[3,2,1,512]{3,2,1,0:T(1,128)S(1)} %get-tuple-element.248), channel_id=1, source_target_pairs={{1,0},{2,1},{3,2},{4,3},{5,4},{6,5},{7,6},{9,8},{10,9},{11,10},{12... | collective-permute-start | bytes 36872 | tf_op jit(solution)/shard_map/ppermute | solution.py:24
  170.4 13.8 %collective-permute-start.15 = (f32[3,2,1,512]{3,2,1,0:T(1,128)S(1)}, f32[3,2,1,512]{3,2,1,0:T(1,128)S(1)}, u32[]{:S(2)}, u32[]{:S(2)}) collective-permute-start(f32[3,2,1,512]{3,2,1,0:T(1,128)S(1)} %get-tuple-element.249), channel_id=1, source_target_pairs={{0,1},{1,2},{2,3},{3,4},{4,5},{5,6},{6,7},{8,9},{9,10},{10,11},{11... | collective-permute-start | bytes 36872 | tf_op jit(solution)/shard_map/ppermute | solution.py:21
  173.5 12.1 %collective-permute-start.12 = (f32[3,1,16,512]{3,2,1,0:T(8,128)S(1)}, f32[3,1,16,512]{3,2,1,0:T(8,128)S(1)}, u32[]{:S(2)}, u32[]{:S(2)}) collective-permute-start(f32[3,1,16,512]{3,2,1,0:T(8,128)S(1)} %get-tuple-element.246), channel_id=1, source_target_pairs={{8,0},{16,8},{24,16},{9,1},{17,9},{25,17},{10,2},{18,10},{26,18},{... | collective-permute-start | bytes 294920 | tf_op jit(solution)/shard_map/ppermute | solution.py:24
  174.8 15.9 %collective-permute-start.13 = (f32[3,1,16,512]{3,2,1,0:T(8,128)S(1)}, f32[3,1,16,512]{3,2,1,0:T(8,128)S(1)}, u32[]{:S(2)}, u32[]{:S(2)}) collective-permute-start(f32[3,1,16,512]{3,2,1,0:T(8,128)S(1)} %get-tuple-element.247), channel_id=1, source_target_pairs={{0,8},{8,16},{16,24},{1,9},{9,17},{17,25},{2,10},{10,18},{18,26},{... | collective-permute-start | bytes 294920 | tf_op jit(solution)/shard_map/ppermute | solution.py:21
  181.4 10.1 %collective-permute-start.11 = (f32[3,2,1,512]{3,2,1,0:T(1,128)S(1)}, f32[3,2,1,512]{3,2,1,0:T(1,128)S(1)}, u32[]{:S(2)}, u32[]{:S(2)}) collective-permute-start(f32[3,2,1,512]{3,2,1,0:T(1,128)S(1)} %get-tuple-element.253), channel_id=1, source_target_pairs={{0,1},{1,2},{2,3},{3,4},{4,5},{5,6},{6,7},{8,9},{9,10},{10,11},{11... | collective-permute-start | bytes 36872 | tf_op jit(solution)/shard_map/ppermute | solution.py:21
  184.2 7.9 %collective-permute-start.8 = (f32[3,1,16,512]{3,2,1,0:T(8,128)S(1)}, f32[3,1,16,512]{3,2,1,0:T(8,128)S(1)}, u32[]{:S(2)}, u32[]{:S(2)}) collective-permute-start(f32[3,1,16,512]{3,2,1,0:T(8,128)S(1)} %get-tuple-element.250), channel_id=1, source_target_pairs={{8,0},{16,8},{24,16},{9,1},{17,9},{25,17},{10,2},{18,10},{26,18},{... | collective-permute-start | bytes 294920 | tf_op jit(solution)/shard_map/ppermute | solution.py:24
  185.5 8.3 %collective-permute-start.9 = (f32[3,1,16,512]{3,2,1,0:T(8,128)S(1)}, f32[3,1,16,512]{3,2,1,0:T(8,128)S(1)}, u32[]{:S(2)}, u32[]{:S(2)}) collective-permute-start(f32[3,1,16,512]{3,2,1,0:T(8,128)S(1)} %get-tuple-element.251), channel_id=1, source_target_pairs={{0,8},{8,16},{16,24},{1,9},{9,17},{17,25},{2,10},{10,18},{18,26},{... | collective-permute-start | bytes 294920 | tf_op jit(solution)/shard_map/ppermute | solution.py:21
  (28 other events, 17.8 us)
Sparse Core Ops, SparseCore 0:
  118.6 132.3 all-reduce.7
where the time goes:
time: 269 us; the launch traced here: 267 us
  waiting for transfers between devices  60.7 us (23%)
  matrix products  50.9 us (19%)
  blocking collectives  44.8 us (17%)
  starting transfers between devices  41.9 us (16%)
  other arithmetic  26.1 us (10%)
  local copies, waits for them, and re-layouts  22.3 us (8%)
  between operations  19.4 us (7%)
    psum x1, waiting for transfers between devices, body(): lax.psum((partials[0], partials[1], partials[2], partials[3], partials[4]...  56.2 us
    psum x1, blocking collectives, body(): lax.psum((partials[0], partials[1], partials[2], partials[3], partials[4]...  44.8 us
    ppermute x8, starting transfers between devices, with_halo(): lax.ppermute(lax.slice_in_dim(block, block.shape[dim] - width, None, axis...  31.2 us
    ppermute x8, starting transfers between devices, with_halo(): lax.ppermute(lax.slice_in_dim(block, 0, width, axis=dim), axis, backward)  10.7 us
    add x32, other arithmetic, backward_step(): left + right  10.1 us
    dot_general x8, matrix products, forward_block(): jnp.dot(w_in, feats, preferred_element_type=jnp.float32) + b_in[:, None]  9.4 us
    slice x8, local copies, waits for them, and re-layouts, forward_block(): b_mid[1][:, None]  6.08 us
    dynamic_update_slice x8, local copies, waits for them, and re-layouts, body(): lax.scan(backward_step, zeros, (feat_blocks, delta_all))  5.41 us
  transfers between devices with their start and end apart: 17, of which 4 were waited for; matrix products, arithmetic and copies ran while one was open for 4% of the time, Pallas kernels for 0%

commit v1 on v0

--- a/solution.py
+++ b/solution.py
@@ -167,9 +167,9 @@
         + (back_y[:, :, 2:] - back_y[:, :, :-2]) * 0.5
         + zdiff(strain_grad[:, 2])
     )
-    summed = lax.psum(
-        (partials[0], partials[1], partials[2], partials[3], partials[4], partials[5]), ("gx", "gy")
-    )
+    summed = (partials[0], partials[1], partials[2], partials[3], partials[4], partials[5])
+    for name in ("gy", "gx"):
+        summed = lax.psum(summed, name)
     total = sum((jnp.sum(jnp.square(item)) for item in summed))
     scale = lax.rsqrt(total / NPARAM + norm_eps)
     results = tuple((item * scale for item in summed))

time: 269 us -> 247 us (0.918)
  waiting for transfers between devices: 60.7 us -> 35.6 us
  blocking collectives: 44.8 us -> 50.1 us
    psum x1 -> x2, waiting for transfers between devices: 56.2 us -> 31.9 us  [body(): summed = lax.psum(summed, name)]
    psum x1 -> x2, blocking collectives: 44.8 us -> 50.1 us  [body(): summed = lax.psum(summed, name)]
  transfers between devices with their start and end apart: 17 -> 18, of which waited for: 4 -> 3; matrix products, arithmetic and copies ran while one was open for 4% -> 5% of each run, Pallas kernels for 0% -> 0%
where the time goes in v1:
time: 247 us; the launch traced here: 245 us
  matrix products  50.9 us (21%)
  blocking collectives  50.1 us (20%)
  starting transfers between devices  39.8 us (16%)
  waiting for transfers between devices  35.6 us (14%)
  other arithmetic  26.1 us (11%)
  local copies, waits for them, and re-layouts  22.3 us (9%)
  between operations  19.4 us (8%)
    psum x2, blocking collectives, body(): summed = lax.psum(summed, name)  50.1 us
    psum x2, waiting for transfers between devices, body(): summed = lax.psum(summed, name)  31.9 us
    ppermute x8, starting transfers between devices, with_halo(): lax.ppermute(lax.slice_in_dim(block, block.shape[dim] - width, None, axis...  29 us
    ppermute x8, starting transfers between devices, with_halo(): lax.ppermute(lax.slice_in_dim(block, 0, width, axis=dim), axis, backward)  10.7 us
    add x32, other arithmetic, backward_step(): left + right  10.1 us
    dot_general x8, matrix products, forward_block(): jnp.dot(w_in, feats, preferred_element_type=jnp.float32) + b_in[:, None]  9.41 us
    slice x8, local copies, waits for them, and re-layouts, forward_block(): b_mid[1][:, None]  6.08 us
    dynamic_update_slice x8, local copies, waits for them, and re-layouts, body(): lax.scan(backward_step, zeros, (feat_blocks, delta_all))  5.42 us
  transfers between devices with their start and end apart: 18, of which 3 were waited for; matrix products, arithmetic and copies ran while one was open for 5% of the time, Pallas kernels for 0%

profile of v1, /device:TPU:0, one launch (start us, length us, event | category | flops | bytes accessed | tf_op | source)
XLA Modules:
  0.0 245.0 jit_solution(13181759675077743735)
XLA Ops:
  7.2 0.9 iota_compare_fusion
  8.2 0.9 fusion.70
  9.1 0.9 fusion.72
  10.2 4.8 %collective-permute-start.1 = (f32[3,1,16,512]{3,2,1,0:T(8,128)S(1)}, f32[3,1,16,512]{3,2,1,0:T(8,128)S(1)}, u32[]{:S(2)}, u32[]{:S(2)}) collective-permute-start(f32[3,1,16,512]{3,2,1,0:T(8,128)S(1)} %get-tuple-element.262), channel_id=1, source_target_pairs={{0,8},{8,16},{16,24},{1,9},{9,17},{17,25},{2,10},{10,18},{18,26},{... | collective-permute-start | bytes 294920 | tf_op jit(solution)/shard_map/ppermute | solution.py:21
  15.1 1.4 collective-permute-start
  16.6 0.8 constant_dynamic-update-slice_fusion.1
  17.4 0.8 fusion.78
  18.2 4.5 %collective-permute-start.5 = (f32[6,1,16,512]{3,2,1,0:T(8,128)}, f32[6,1,16,512]{3,2,1,0:T(8,128)S(1)}, u32[]{:S(2)}, u32[]{:S(2)}) collective-permute-start(f32[6,1,16,512]{3,2,1,0:T(8,128)} %get-tuple-element.245), channel_id=1, source_target_pairs={{0,8},{8,16},{16,24},{1,9},{9,17},{17,25},{2,10},{10,18},{18,26},{... | collective-permute-start | bytes 589832 | tf_op jit(solution)/shard_map/ppermute | solution.py:21
  22.7 1.3 collective-permute-start.4
  24.8 1.3 collective-permute-start.2
  26.1 3.0 %collective-permute-start.3 = (f32[3,4,1,512]{3,2,1,0:T(1,128)S(1)}, f32[3,4,1,512]{3,2,1,0:T(1,128)S(1)}, u32[]{:S(2)}, u32[]{:S(2)}) collective-permute-start(f32[3,4,1,512]{3,2,1,0:T(1,128)S(1)} %get-tuple-element.250), channel_id=1, source_target_pairs={{0,1},{1,2},{2,3},{3,4},{4,5},{5,6},{6,7},{8,9},{9,10},{10,11},{11... | collective-permute-start | bytes 73736 | tf_op jit(solution)/shard_map/ppermute | solution.py:21
  31.3 2.3 collective-permute-done.4
  33.7 1.4 collective-permute-start.6
  35.1 3.0 %collective-permute-start.7 = (f32[6,4,1,512]{3,2,1,0:T(1,128)S(1)}, f32[6,4,1,512]{3,2,1,0:T(1,128)S(1)}, u32[]{:S(2)}, u32[]{:S(2)}) collective-permute-start(f32[6,4,1,512]{3,2,1,0:T(1,128)S(1)} %get-tuple-element.238), channel_id=1, source_target_pairs={{0,1},{1,2},{2,3},{3,4},{4,5},{5,6},{6,7},{8,9},{9,10},{10,11},{11... | collective-permute-start | bytes 147464 | tf_op jit(solution)/shard_map/ppermute | solution.py:21
  38.1 0.9 multiply_bitcast_fusion
  40.5 76.0 %while.25 = (s32[]{:T(128)}, f32[256,10]{0,1:T(8,128)S(1)}, f32[256]{0:T(256)}, f32[2,256,256]{2,1,0:T(8,128)S(1)}, f32[2,256]{1,0:T(2,128)}, /*index=5*/f32[9,2...) while((s32[]{:T(128)}, f32[256,10]{0,1:T(8,128)S(1)}, ...), condition=%wide.region_5.6_spmd.clone, body=%wide.region_0.5_spmd.clone.sunk | while | flops 1684996864 | bytes 26539676 | solution.py:145
  40.5 0.8 fusion.150
  42.0 1.2 fusion.149
  48.8 0.7 fusion.154
  49.4 0.8 fusion.150
  50.4 1.2 fusion.153
  51.6 1.2 fusion.149
  58.3 0.7 fusion.154
  59.0 0.8 fusion.150
  60.0 1.2 fusion.153
  61.2 1.2 fusion.149
  67.9 0.7 fusion.154
  68.6 0.8 fusion.150
  69.6 1.2 fusion.153
  70.7 1.2 fusion.149
  77.5 0.7 fusion.154
  78.2 0.8 fusion.150
  79.2 1.2 fusion.153
  80.3 1.2 fusion.149
  87.1 0.7 fusion.154
  87.8 0.8 fusion.150
  88.8 1.2 fusion.153
  89.9 1.2 fusion.149
  96.7 0.7 fusion.154
  97.4 0.8 fusion.150
  98.3 1.2 fusion.153
  99.5 1.2 fusion.149
  106.3 0.7 fusion.154
  106.9 0.8 fusion.150
  107.9 1.2 fusion.153
  109.1 1.2 fusion.149
  115.8 0.7 fusion.154
  118.6 1.3 collective-permute-start.10
  119.9 33.0 %all-reduce.5 = (f32[256,10]{0,1:T(8,128)S(1)}, f32[256]{0:T(256)S(1)}, f32[2,256]{1,0:T(2,128)S(1)}, f32[9,256]{1,0:T(8,128)S(1)}, f32[9]{0:T(128)S(1)}) all-reduce(f32[256,10]{0,1:T(8,128)S(1)} %copy-done.11, f32[256]{0:T(256)S(1)} %copy-done.29, f32[2,256]{1,0:T(2,128)S(1)} %copy-done.25, ...), channel_id=1, replica_groups=mesh['gx'=4,'gy'=8] {'gy'}, use_global_device_ids=true, to_apply=%region_6.7 | all-reduce | flops 5641 | bytes 45128 | tf_op jit(solution)/shard_map/psum | solution.py:172
  152.9 17.2 %all-reduce.6 = (f32[256,10]{0,1:T(8,128)S(1)}, f32[256]{0:T(256)S(1)}, f32[2,256]{1,0:T(2,128)S(1)}, f32[9,256]{1,0:T(8,128)S(1)}, f32[9]{0:T(128)S(1)}) all-reduce(f32[256,10]{0,1:T(8,128)S(1)} %get-tuple-element.215, f32[256]{0:T(256)S(1)} %get-tuple-element.216, ...), channel_id=1, replica_groups=mesh['gx'=4,'gy'=8] {'gx'}, use_global_device_ids=true, to_apply=%region_7.8 | all-reduce | flops 5641 | bytes 45128 | tf_op jit(solution)/shard_map/psum | solution.py:172
  171.9 1.6 copy.28
  173.7 1.3 collective-permute-start.14
  175.0 3.0 %collective-permute-start.15 = (f32[3,2,1,512]{3,2,1,0:T(1,128)S(1)}, f32[3,2,1,512]{3,2,1,0:T(1,128)S(1)}, u32[]{:S(2)}, u32[]{:S(2)}) collective-permute-start(f32[3,2,1,512]{3,2,1,0:T(1,128)S(1)} %get-tuple-element.254), channel_id=1, source_target_pairs={{0,1},{1,2},{2,3},{3,4},{4,5},{5,6},{6,7},{8,9},{9,10},{10,11},{11... | collective-permute-start | bytes 36872 | tf_op jit(solution)/shard_map/ppermute | solution.py:21
  178.1 1.4 collective-permute-start.12
  179.5 4.6 %collective-permute-start.13 = (f32[3,1,16,512]{3,2,1,0:T(8,128)S(1)}, f32[3,1,16,512]{3,2,1,0:T(8,128)S(1)}, u32[]{:S(2)}, u32[]{:S(2)}) collective-permute-start(f32[3,1,16,512]{3,2,1,0:T(8,128)S(1)} %get-tuple-element.252), channel_id=1, source_target_pairs={{0,8},{8,16},{16,24},{1,9},{9,17},{17,25},{2,10},{10,18},{18,26},{... | collective-permute-start | bytes 294920 | tf_op jit(solution)/shard_map/ppermute | solution.py:21
  186.7 1.4 collective-permute-start.11
  188.1 1.3 collective-permute-start.8
  189.4 4.6 %collective-permute-start.9 = (f32[3,1,16,512]{3,2,1,0:T(8,128)S(1)}, f32[3,1,16,512]{3,2,1,0:T(8,128)S(1)}, u32[]{:S(2)}, u32[]{:S(2)}) collective-permute-start(f32[3,1,16,512]{3,2,1,0:T(8,128)S(1)} %get-tuple-element.256), channel_id=1, source_target_pairs={{0,8},{8,16},{16,24},{1,9},{9,17},{17,25},{2,10},{10,18},{18,26},{... | collective-permute-start | bytes 294920 | tf_op jit(solution)/shard_map/ppermute | solution.py:21
  193.9 0.9 fusion.49
  194.8 1.3 collective-permute-done.9
  196.2 1.0 fusion.42
  197.1 31.9 %all-reduce.12.cloned.1.call-done = f32[2,256,256]{2,1,0:T(8,128)} async-done(((f32[2,256,256]{2,1,0:T(8,128)}), f32[2,256,256]{2,1,0:T(8,128)}) %all-reduce.12.cloned.1.call-update) | async-done | bytes 524304 | tf_op jit(solution)/shard_map/psum | solution.py:172
  229.0 1.8 multiply_reduce_fusion
  236.3 1.9 broadcast_multiply_fusion.1
  (347 shorter events, 58.1 us)
Async XLA Ops:
  7.2 2.9 %copy-start.13 = (s32[2,16,512]{2,1,0:T(8,128)S(1)}, s32[2,16,512]{2,1,0:T(8,128)}, u32[]{:S(2)}) copy-start(s32[2,16,512]{2,1,0:T(8,128)} %param.15) | copy-start | bytes 196612
  7.2 3.0 %copy-start.20 = (f32[3,2,16,512]{3,2,1,0:T(8,128)S(1)}, f32[3,2,16,512]{3,2,1,0:T(8,128)}, u32[]{:S(2)}) copy-start(f32[3,2,16,512]{3,2,1,0:T(8,128)} %param.20) | copy-start | bytes 589828
  7.2 177.0 %all-reduce.10.cloned.1.call-start = ((), (), s32[]{:S(2)}) async-start(), calls=%async_computation | async-start | bytes 1048576 | tf_op jit(solution)/shard_map/psum | solution.py:172
  8.2 8.4 %copy-start.21 = (f32[3,2,16,512]{3,2,1,0:T(8,128)S(1)}, f32[3,2,16,512]{3,2,1,0:T(8,128)}, u32[]{:S(2)}) copy-start(f32[3,2,16,512]{3,2,1,0:T(8,128)} %param.18) | copy-start | bytes 589828
  9.1 8.3 %copy-start.1 = (f32[3,2,16,512]{3,2,1,0:T(8,128)S(1)}, f32[3,2,16,512]{3,2,1,0:T(8,128)}, u32[]{:S(2)}) copy-start(f32[3,2,16,512]{3,2,1,0:T(8,128)} %param.19) | copy-start | bytes 589828
  10.1 5.0 %copy-start.7 = (f32[1,2,16,512]{3,2,1,0:T(8,128)}, f32[1,2,16,512]{3,2,1,0:T(8,128)S(1)}, u32[]{:S(2)}) copy-start(f32[1,2,16,512]{3,2,1,0:T(8,128)S(1)} %copy.58) | copy-start | bytes 196612
  10.1 19.9 %copy-start.3 = (f32[2,16,512]{2,1,0:T(8,128)}, f32[2,16,512]{2,1,0:T(8,128)S(1)}, u32[]{:S(2)}) copy-start(f32[2,16,512]{2,1,0:T(8,128)S(1)} %get-tuple-element.225) | copy-start | bytes 196612
  10.2 5.0 %copy-start.5 = (f32[2,16,512]{2,1,0:T(8,128)}, f32[2,16,512]{2,1,0:T(8,128)S(1)}, u32[]{:S(2)}) copy-start(f32[2,16,512]{2,1,0:T(8,128)S(1)} %broadcast_select_fusion.1) | copy-start | bytes 196612
  10.2 14.4 %collective-permute-start.1 = (f32[3,1,16,512]{3,2,1,0:T(8,128)S(1)}, f32[3,1,16,512]{3,2,1,0:T(8,128)S(1)}, u32[]{:S(2)}, u32[]{:S(2)}) collective-permute-start(f32[3,1,16,512]{3,2,1,0:T(8,128)S(1)} %get-tuple-element.262), channel_id=1, source_target_pairs={{0,8},{8,16},{16,24},{1,9},{9,17},{17,25},{2,10},{10,18},{18,26},{... | collective-permute-start | bytes 294920 | tf_op jit(solution)/shard_map/ppermute | solution.py:21
  15.1 14.0 %copy-start.26 = (s32[2,16,512]{2,1,0:T(8,128)S(1)}, s32[2,16,512]{2,1,0:T(8,128)}, u32[]{:S(2)}) copy-start(s32[2,16,512]{2,1,0:T(8,128)} %param.16) | copy-start | bytes 196612
  15.1 9.6 %collective-permute-start = (f32[3,1,16,512]{3,2,1,0:T(8,128)S(1)}, f32[3,1,16,512]{3,2,1,0:T(8,128)S(1)}, u32[]{:S(2)}, u32[]{:S(2)}) collective-permute-start(f32[3,1,16,512]{3,2,1,0:T(8,128)S(1)} %get-tuple-element.263), channel_id=1, source_target_pairs={{8,0},{16,8},{24,16},{9,1},{17,9},{25,17},{10,2},{18,10},{26,18},{... | collective-permute-start | bytes 294920 | tf_op jit(solution)/shard_map/ppermute | solution.py:24
  18.2 13.1 %collective-permute-start.5 = (f32[6,1,16,512]{3,2,1,0:T(8,128)}, f32[6,1,16,512]{3,2,1,0:T(8,128)S(1)}, u32[]{:S(2)}, u32[]{:S(2)}) collective-permute-start(f32[6,1,16,512]{3,2,1,0:T(8,128)} %get-tuple-element.245), channel_id=1, source_target_pairs={{0,8},{8,16},{16,24},{1,9},{9,17},{17,25},{2,10},{10,18},{18,26},{... | collective-permute-start | bytes 589832 | tf_op jit(solution)/shard_map/ppermute | solution.py:21
  22.7 10.8 %collective-permute-start.4 = (f32[6,1,16,512]{3,2,1,0:T(8,128)}, f32[6,1,16,512]{3,2,1,0:T(8,128)S(1)}, u32[]{:S(2)}, u32[]{:S(2)}) collective-permute-start(f32[6,1,16,512]{3,2,1,0:T(8,128)} %get-tuple-element.246), channel_id=1, source_target_pairs={{8,0},{16,8},{24,16},{9,1},{17,9},{25,17},{10,2},{18,10},{26,18},{... | collective-permute-start | bytes 589832 | tf_op jit(solution)/shard_map/ppermute | solution.py:24
  24.8 6.0 %collective-permute-start.2 = (f32[3,4,1,512]{3,2,1,0:T(1,128)S(1)}, f32[3,4,1,512]{3,2,1,0:T(1,128)S(1)}, u32[]{:S(2)}, u32[]{:S(2)}) collective-permute-start(f32[3,4,1,512]{3,2,1,0:T(1,128)S(1)} %get-tuple-element.249), channel_id=1, source_target_pairs={{1,0},{2,1},{3,2},{4,3},{5,4},{6,5},{7,6},{9,8},{10,9},{11,10},{12... | collective-permute-start | bytes 73736 | tf_op jit(solution)/shard_map/ppermute | solution.py:24
  26.1 4.7 %collective-permute-start.3 = (f32[3,4,1,512]{3,2,1,0:T(1,128)S(1)}, f32[3,4,1,512]{3,2,1,0:T(1,128)S(1)}, u32[]{:S(2)}, u32[]{:S(2)}) collective-permute-start(f32[3,4,1,512]{3,2,1,0:T(1,128)S(1)} %get-tuple-element.250), channel_id=1, source_target_pairs={{0,1},{1,2},{2,3},{3,4},{4,5},{5,6},{6,7},{8,9},{9,10},{10,11},{11... | collective-permute-start | bytes 73736 | tf_op jit(solution)/shard_map/ppermute | solution.py:21
  33.7 6.0 %copy-start.12 = (bf16[3,1,2,16,512]{4,3,2,0,1:T(8,128)(2,1)S(1)}, bf16[3,1,2,16,512]{4,3,2,0,1:T(8,128)(2,1)}, u32[]{:S(2)}) copy-start(bf16[3,1,2,16,512]{4,3,2,0,1:T(8,128)(2,1)} %get-tuple-element.260) | copy-start | bytes 294916
  33.7 5.4 %collective-permute-start.6 = (f32[6,4,1,512]{3,2,1,0:T(1,128)S(1)}, f32[6,4,1,512]{3,2,1,0:T(1,128)S(1)}, u32[]{:S(2)}, u32[]{:S(2)}) collective-permute-start(f32[6,4,1,512]{3,2,1,0:T(1,128)S(1)} %get-tuple-element.237), channel_id=1, source_target_pairs={{1,0},{2,1},{3,2},{4,3},{5,4},{6,5},{7,6},{9,8},{10,9},{11,10},{12... | collective-permute-start | bytes 147464 | tf_op jit(solution)/shard_map/ppermute | solution.py:24
  35.1 3.9 %collective-permute-start.7 = (f32[6,4,1,512]{3,2,1,0:T(1,128)S(1)}, f32[6,4,1,512]{3,2,1,0:T(1,128)S(1)}, u32[]{:S(2)}, u32[]{:S(2)}) collective-permute-start(f32[6,4,1,512]{3,2,1,0:T(1,128)S(1)} %get-tuple-element.238), channel_id=1, source_target_pairs={{0,1},{1,2},{2,3},{3,4},{4,5},{5,6},{6,7},{8,9},{9,10},{10,11},{11... | collective-permute-start | bytes 147464 | tf_op jit(solution)/shard_map/ppermute | solution.py:21
  39.2 0.8 copy-start.22
  39.8 0.7 copy-start.9
  39.8 0.7 copy-start.14
  39.8 0.7 copy-start.15
  40.5 2.7 %copy-start.32 = (bf16[2,256,256]{2,1,0:T(8,128)(2,1)S(1)}, bf16[2,256,256]{2,1,0:T(8,128)(2,1)}, u32[]{:S(2)}) copy-start(bf16[2,256,256]{2,1,0:T(8,128)(2,1)} %get-tuple-element.435) | copy-start | bytes 786436 | tf_op jit(solution)/shard_map/while
  45.9 0.7 copy-start.23
  46.6 1.1 copy-start.24
  49.4 3.4 %copy-start.32 = (bf16[2,256,256]{2,1,0:T(8,128)(2,1)S(1)}, bf16[2,256,256]{2,1,0:T(8,128)(2,1)}, u32[]{:S(2)}) copy-start(bf16[2,256,256]{2,1,0:T(8,128)(2,1)} %get-tuple-element.435) | copy-start | bytes 786436 | tf_op jit(solution)/shard_map/while
  55.5 0.7 copy-start.23
  56.2 1.1 copy-start.24
  59.0 3.3 %copy-start.32 = (bf16[2,256,256]{2,1,0:T(8,128)(2,1)S(1)}, bf16[2,256,256]{2,1,0:T(8,128)(2,1)}, u32[]{:S(2)}) copy-start(bf16[2,256,256]{2,1,0:T(8,128)(2,1)} %get-tuple-element.435) | copy-start | bytes 786436 | tf_op jit(solution)/shard_map/while
  65.1 0.7 copy-start.23
  65.8 1.1 copy-start.24
  68.6 3.4 %copy-start.32 = (bf16[2,256,256]{2,1,0:T(8,128)(2,1)S(1)}, bf16[2,256,256]{2,1,0:T(8,128)(2,1)}, u32[]{:S(2)}) copy-start(bf16[2,256,256]{2,1,0:T(8,128)(2,1)} %get-tuple-element.435) | copy-start | bytes 786436 | tf_op jit(solution)/shard_map/while
  74.7 0.7 copy-start.23
  75.4 1.1 copy-start.24
  78.2 3.3 %copy-start.32 = (bf16[2,256,256]{2,1,0:T(8,128)(2,1)S(1)}, bf16[2,256,256]{2,1,0:T(8,128)(2,1)}, u32[]{:S(2)}) copy-start(bf16[2,256,256]{2,1,0:T(8,128)(2,1)} %get-tuple-element.435) | copy-start | bytes 786436 | tf_op jit(solution)/shard_map/while
  84.3 0.7 copy-start.23
  85.0 1.1 copy-start.24
  87.8 3.3 %copy-start.32 = (bf16[2,256,256]{2,1,0:T(8,128)(2,1)S(1)}, bf16[2,256,256]{2,1,0:T(8,128)(2,1)}, u32[]{:S(2)}) copy-start(bf16[2,256,256]{2,1,0:T(8,128)(2,1)} %get-tuple-element.435) | copy-start | bytes 786436 | tf_op jit(solution)/shard_map/while
  93.9 0.7 copy-start.23
  94.6 1.1 copy-start.24
  97.4 3.3 %copy-start.32 = (bf16[2,256,256]{2,1,0:T(8,128)(2,1)S(1)}, bf16[2,256,256]{2,1,0:T(8,128)(2,1)}, u32[]{:S(2)}) copy-start(bf16[2,256,256]{2,1,0:T(8,128)(2,1)} %get-tuple-element.435) | copy-start | bytes 786436 | tf_op jit(solution)/shard_map/while
  104.1 1.1 copy-start.24
  106.9 3.3 %copy-start.32 = (bf16[2,256,256]{2,1,0:T(8,128)(2,1)S(1)}, bf16[2,256,256]{2,1,0:T(8,128)(2,1)}, u32[]{:S(2)}) copy-start(bf16[2,256,256]{2,1,0:T(8,128)(2,1)} %get-tuple-element.435) | copy-start | bytes 786436 | tf_op jit(solution)/shard_map/while
  113.7 1.1 copy-start.24
  116.5 1.1 copy-start
  117.5 0.8 copy-start.4
  118.4 1.5 copy-start.11
  118.4 1.5 copy-start.25
  118.4 1.5 copy-start.29
  118.4 1.5 copy-start.30
  118.5 110.5 %all-reduce.12.cloned.1.call-start = ((), (), s32[]{:S(2)}) async-start(), calls=%async_computation.1 | async-start | bytes 1048576 | tf_op jit(solution)/shard_map/psum | solution.py:172
  118.6 76.2 %collective-permute-start.10 = (f32[3,2,1,512]{3,2,1,0:T(1,128)S(1)}, f32[3,2,1,512]{3,2,1,0:T(1,128)S(1)}, u32[]{:S(2)}, u32[]{:S(2)}) collective-permute-start(f32[3,2,1,512]{3,2,1,0:T(1,128)S(1)} %get-tuple-element.257), channel_id=1, source_target_pairs={{1,0},{2,1},{3,2},{4,3},{5,4},{6,5},{7,6},{9,8},{10,9},{11,10},{12... | collective-permute-start | bytes 36872 | tf_op jit(solution)/shard_map/ppermute | solution.py:24
  173.7 13.0 %collective-permute-start.14 = (f32[3,2,1,512]{3,2,1,0:T(1,128)S(1)}, f32[3,2,1,512]{3,2,1,0:T(1,128)S(1)}, u32[]{:S(2)}, u32[]{:S(2)}) collective-permute-start(f32[3,2,1,512]{3,2,1,0:T(1,128)S(1)} %get-tuple-element.253), channel_id=1, source_target_pairs={{1,0},{2,1},{3,2},{4,3},{5,4},{6,5},{7,6},{9,8},{10,9},{11,10},{12... | collective-permute-start | bytes 36872 | tf_op jit(solution)/shard_map/ppermute | solution.py:24
  175.0 13.1 %collective-permute-start.15 = (f32[3,2,1,512]{3,2,1,0:T(1,128)S(1)}, f32[3,2,1,512]{3,2,1,0:T(1,128)S(1)}, u32[]{:S(2)}, u32[]{:S(2)}) collective-permute-start(f32[3,2,1,512]{3,2,1,0:T(1,128)S(1)} %get-tuple-element.254), channel_id=1, source_target_pairs={{0,1},{1,2},{2,3},{3,4},{4,5},{5,6},{6,7},{8,9},{9,10},{10,11},{11... | collective-permute-start | bytes 36872 | tf_op jit(solution)/shard_map/ppermute | solution.py:21
  178.1 18.1 %copy-start.2 = (f32[3,2,16,512]{3,2,1,0:T(8,128)S(1)}, f32[3,2,16,512]{3,2,1,0:T(8,128)}, u32[]{:S(2)}) copy-start(f32[3,2,16,512]{3,2,1,0:T(8,128)} %param.19) | copy-start | bytes 589828
  178.1 18.1 %copy-start.6 = (f32[2,16,512]{2,1,0:T(8,128)S(1)}, f32[2,16,512]{2,1,0:T(8,128)}, u32[]{:S(2)}) copy-start(f32[2,16,512]{2,1,0:T(8,128)} %copy-done.5) | copy-start | bytes 196612
  178.1 18.1 %copy-start.8 = (f32[1,2,16,512]{3,2,1,0:T(8,128)S(1)}, f32[1,2,16,512]{3,2,1,0:T(8,128)}, u32[]{:S(2)}) copy-start(f32[1,2,16,512]{3,2,1,0:T(8,128)} %copy-done.7) | copy-start | bytes 196612
  178.1 18.0 %copy-start.17 = (f32[6,4,1,512]{3,2,1,0:T(1,128)S(1)}, f32[6,4,1,512]{3,2,1,0:T(1,128)}, u32[]{:S(2)}) copy-start(f32[6,4,1,512]{3,2,1,0:T(1,128)} %copy-done.16) | copy-start | bytes 147460
  178.1 18.0 %copy-start.19 = (f32[6,4,1,512]{3,2,1,0:T(1,128)S(1)}, f32[6,4,1,512]{3,2,1,0:T(1,128)}, u32[]{:S(2)}) copy-start(f32[6,4,1,512]{3,2,1,0:T(1,128)} %copy-done.18) | copy-start | bytes 147460
  178.1 11.3 %collective-permute-start.12 = (f32[3,1,16,512]{3,2,1,0:T(8,128)S(1)}, f32[3,1,16,512]{3,2,1,0:T(8,128)S(1)}, u32[]{:S(2)}, u32[]{:S(2)}) collective-permute-start(f32[3,1,16,512]{3,2,1,0:T(8,128)S(1)} %get-tuple-element.251), channel_id=1, source_target_pairs={{8,0},{16,8},{24,16},{9,1},{17,9},{25,17},{10,2},{18,10},{26,18},{... | collective-permute-start | bytes 294920 | tf_op jit(solution)/shard_map/ppermute | solution.py:24
  179.5 14.4 %collective-permute-start.13 = (f32[3,1,16,512]{3,2,1,0:T(8,128)S(1)}, f32[3,1,16,512]{3,2,1,0:T(8,128)S(1)}, u32[]{:S(2)}, u32[]{:S(2)}) collective-permute-start(f32[3,1,16,512]{3,2,1,0:T(8,128)S(1)} %get-tuple-element.252), channel_id=1, source_target_pairs={{0,8},{8,16},{16,24},{1,9},{9,17},{17,25},{2,10},{10,18},{18,26},{... | collective-permute-start | bytes 294920 | tf_op jit(solution)/shard_map/ppermute | solution.py:21
  186.7 8.1 %collective-permute-start.11 = (f32[3,2,1,512]{3,2,1,0:T(1,128)S(1)}, f32[3,2,1,512]{3,2,1,0:T(1,128)S(1)}, u32[]{:S(2)}, u32[]{:S(2)}) collective-permute-start(f32[3,2,1,512]{3,2,1,0:T(1,128)S(1)} %get-tuple-element.258), channel_id=1, source_target_pairs={{0,1},{1,2},{2,3},{3,4},{4,5},{5,6},{6,7},{8,9},{9,10},{10,11},{11... | collective-permute-start | bytes 36872 | tf_op jit(solution)/shard_map/ppermute | solution.py:21
  188.1 6.7 %collective-permute-start.8 = (f32[3,1,16,512]{3,2,1,0:T(8,128)S(1)}, f32[3,1,16,512]{3,2,1,0:T(8,128)S(1)}, u32[]{:S(2)}, u32[]{:S(2)}) collective-permute-start(f32[3,1,16,512]{3,2,1,0:T(8,128)S(1)} %get-tuple-element.255), channel_id=1, source_target_pairs={{8,0},{16,8},{24,16},{9,1},{17,9},{25,17},{10,2},{18,10},{26,18},{... | collective-permute-start | bytes 294920 | tf_op jit(solution)/shard_map/ppermute | solution.py:24
  189.4 6.8 %collective-permute-start.9 = (f32[3,1,16,512]{3,2,1,0:T(8,128)S(1)}, f32[3,1,16,512]{3,2,1,0:T(8,128)S(1)}, u32[]{:S(2)}, u32[]{:S(2)}) collective-permute-start(f32[3,1,16,512]{3,2,1,0:T(8,128)S(1)} %get-tuple-element.256), channel_id=1, source_target_pairs={{0,8},{8,16},{16,24},{1,9},{9,17},{17,25},{2,10},{10,18},{18,26},{... | collective-permute-start | bytes 294920 | tf_op jit(solution)/shard_map/ppermute | solution.py:21
  (29 other events, 18.5 us)
Sparse Core Ops, SparseCore 0:
  118.6 60.5 all-reduce.9
  184.3 44.6 all-reduce.11
